TPU v7x, 128 devices: a whole 4x4x4 slice. The times are simulated.
128 devices in a mesh: row: 8 (over z_lo, y), col: 16 (over x, z_hi, core).
Axes of the slice: x: 4, y: 4, z: 4 (z_hi: 2, z_lo: 2; z = z_hi * 2 + z_lo), core: 2. Of those that a mesh axis runs over, the one named last changes fastest.
Arguments:
- single: bfloat16 [2048, 384], P(('row', 'col')), may hold values from -6 to 6
- pair_input: bfloat16 [2048, 2048, 128], P('row', 'col'), may hold values from -6 to 6
- segment_lengths: int32 [8], replicated, may hold values from 1 to 512, 2048 in all
- single_gain: float32 [384], replicated, may hold values from 0.5 to 1.5
- w_left: bfloat16 [384, 32], replicated, may hold values from -0.3125 to 0.3125
- w_right: bfloat16 [384, 32], replicated, may hold values from -0.3125 to 0.3125
- w_outer: bfloat16 [1024, 128], replicated, may hold values from -0.1875 to 0.1875
- pair_gain: float32 [128], replicated, may hold values from 0.5 to 1.5
- w_gate: bfloat16 [128, 512], replicated, may hold values from -0.5 to 0.5
- w_up: bfloat16 [128, 512], replicated, may hold values from -0.5 to 0.5
- w_down: bfloat16 [512, 128], replicated, may hold values from -0.25 to 0.25
- bias_gain: float32 [128], replicated, may hold values from 0.5 to 1.5
- w_bias: bfloat16 [128, 16], replicated, may hold values from -8 to 8
- w_query: bfloat16 [384, 384], replicated, may hold values from -0.3125 to 0.3125
- w_key: bfloat16 [384, 384], replicated, may hold values from -0.3125 to 0.3125
- w_value: bfloat16 [384, 384], replicated, may hold values from -0.3125 to 0.3125
- w_gate_attn: bfloat16 [384, 384], replicated, may hold values from -0.3125 to 0.3125
- w_output: bfloat16 [384, 384], replicated, may hold values from -0.3125 to 0.3125
Outputs:
- single_out: bfloat16 [2048, 384], P(('row', 'col'))
- pair_out: bfloat16 [2048, 2048, 128], P('row', 'col')
Inputs may be any that keep to these rules, and one draw needn't show every extreme that they name: `segment_lengths`: the last entry is the number of padding tokens at the end of the window; the others are chain lengths.
All inputs are finite; a program needn't handle non-finite values.
Results may differ from a plain program's by a relative error of at most 0.0085.
The roundings to bfloat16 on the way count: a program that leaves them out, or rounds other values in their place, can miss the bound.
Values may be sent and summed in bfloat16 or wider, within the bound.
A program may use at most 128 MiB of HBM per device.

v0:
```python
import math
import jax
import jax.numpy as jnp
from jax import lax
from jax.sharding import PartitionSpec as P

EPSILON = 1e-05


def normalize(values, gain_vector):
    average = jnp.mean(values, -1, keepdims=True)
    centered = values - average
    variance = jnp.mean(centered * centered, -1, keepdims=True)
    return centered * lax.rsqrt(variance + EPSILON) * gain_vector


def matmul(left_side, right_side):
    return jnp.dot(left_side, right_side, preferred_element_type=jnp.float32)


def on_device(
    single,
    pair_input,
    segment_lengths,
    single_gain,
    w_left,
    w_right,
    w_outer,
    pair_gain,
    w_gate,
    w_up,
    w_down,
    bias_gain,
    w_bias,
    w_query,
    w_key,
    w_value,
    w_gate_attn,
    w_output,
):
    row_count = pair_input.shape[0]
    col_count = pair_input.shape[1]
    pair_width = pair_input.shape[2]
    own_count = single.shape[0]
    single_width = single.shape[1]
    head_count = w_bias.shape[1]
    head_dim = single_width // head_count
    outer_width = w_left.shape[1]
    row_devices = lax.axis_size("row")
    row_index = lax.axis_index("row")
    col_index = lax.axis_index("col")
    token_total = row_count * row_devices
    valid_limit = token_total - segment_lengths[segment_lengths.shape[0] - 1]
    row_start = row_index * row_count
    col_start = col_index * col_count

    def alive_mask(first_token, length):
        return (first_token + jnp.arange(length, dtype=jnp.int32) < valid_limit).astype(
            jnp.float32
        )[:, None]

    own_norm = normalize(single.astype(jnp.float32), single_gain).astype(jnp.bfloat16)
    gate_lin = matmul(own_norm, w_gate_attn)
    everything = lax.all_gather(single, ("row", "col"), axis=0, tiled=True)
    row_norm = normalize(
        lax.dynamic_slice_in_dim(everything, row_start, row_count, 0).astype(jnp.float32),
        single_gain,
    ).astype(jnp.bfloat16)
    col_norm = normalize(
        lax.dynamic_slice_in_dim(everything, col_start, col_count, 0).astype(jnp.float32),
        single_gain,
    ).astype(jnp.bfloat16)
    left_rows = (matmul(row_norm, w_left) * alive_mask(row_start, row_count)).astype(jnp.bfloat16)
    query_rows = matmul(row_norm, w_query).astype(jnp.bfloat16)
    right_cols = (matmul(col_norm, w_right) * alive_mask(col_start, col_count)).astype(jnp.bfloat16)
    key_cols = matmul(col_norm, w_key).astype(jnp.bfloat16)
    value_cols = matmul(col_norm, w_value).astype(jnp.bfloat16)
    outer_table = w_outer.reshape(outer_width, outer_width, pair_width)
    right_table = jnp.einsum(
        "jd,cdz->cjz", right_cols, outer_table, preferred_element_type=jnp.float32
    ).astype(jnp.bfloat16)
    right_table = right_table.reshape(outer_width, col_count * pair_width)
    keys_head = key_cols.reshape(col_count, head_count, head_dim)
    values_head = value_cols.reshape(col_count, head_count, head_dim)
    col_alive = col_start + jnp.arange(col_count, dtype=jnp.int32) < valid_limit
    score_scale = 1.0 / math.sqrt(head_dim)
    block_rows = math.gcd(row_count, 32)
    block_total = row_count // block_rows

    def one_block(offset):
        left_block = lax.dynamic_slice_in_dim(left_rows, offset, block_rows, 0)
        pair_block = lax.dynamic_slice_in_dim(pair_input, offset, block_rows, 0)
        middle = pair_block.astype(jnp.float32) + matmul(left_block, right_table).reshape(
            block_rows, col_count, pair_width
        )
        normed = (
            normalize(middle, pair_gain)
            .astype(jnp.bfloat16)
            .reshape(block_rows * col_count, pair_width)
        )
        hidden = (jax.nn.silu(matmul(normed, w_gate)) * matmul(normed, w_up)).astype(jnp.bfloat16)
        new_pair = (
            middle + matmul(hidden, w_down).reshape(block_rows, col_count, pair_width)
        ).astype(jnp.bfloat16)
        bias_input = (
            normalize(new_pair.astype(jnp.float32), bias_gain)
            .astype(jnp.bfloat16)
            .reshape(block_rows * col_count, pair_width)
        )
        pair_bias = matmul(bias_input, w_bias).reshape(block_rows, col_count, head_count)
        query_block = lax.dynamic_slice_in_dim(query_rows, offset, block_rows, 0).reshape(
            block_rows, head_count, head_dim
        )
        scores = (
            jnp.einsum("ihd,jhd->hij", query_block, keys_head, preferred_element_type=jnp.float32)
            * score_scale
        )
        scores = scores + jnp.transpose(pair_bias, (2, 0, 1))
        scores = jnp.where(col_alive[None, None, :], scores, -1e30)
        return (new_pair, scores)

    offsets = jnp.arange(block_total, dtype=jnp.int32) * block_rows
    new_pairs, scores = lax.map(one_block, offsets)
    pair_out = new_pairs.reshape(row_count, col_count, pair_width)
    local_peak = jnp.transpose(jnp.max(scores, -1), (0, 2, 1)).reshape(row_count, head_count)
    row_peak = lax.pmax(local_peak, "col")
    peak_blocks = jnp.transpose(row_peak.reshape(block_total, block_rows, head_count), (0, 2, 1))
    weights = jnp.exp(scores - peak_blocks[..., None])
    denominator = jnp.transpose(jnp.sum(weights, -1), (0, 2, 1)).reshape(row_count, head_count)
    numerator = jnp.einsum(
        "bhij,jhd->bihd",
        weights.astype(jnp.bfloat16),
        values_head,
        preferred_element_type=jnp.float32,
    )
    numerator = numerator.reshape(row_count, single_width)
    numerator, denominator = (
        lax.psum(numerator.astype(jnp.bfloat16), "col").astype(jnp.float32),
        lax.psum(denominator.astype(jnp.bfloat16), "col").astype(jnp.float32),
    )
    own_rows = col_index * own_count
    numerator = lax.dynamic_slice_in_dim(numerator, own_rows, own_count, 0)
    denominator = lax.dynamic_slice_in_dim(denominator, own_rows, own_count, 0)
    attended = (
        numerator.reshape(own_count, head_count, head_dim) / denominator[:, :, None]
    ).reshape(own_count, single_width)
    gated = (jax.nn.sigmoid(gate_lin) * attended).astype(jnp.bfloat16)
    single_out = (single.astype(jnp.float32) + matmul(gated, w_output)).astype(jnp.bfloat16)
    return (single_out, pair_out)


def solution(mesh):
    in_specs = (
        P(("row", "col"), None),
        P("row", "col", None),
        P(),
        P(),
        P(),
        P(),
        P(),
        P(),
        P(),
        P(),
        P(),
        P(),
        P(),
        P(),
        P(),
        P(),
        P(),
        P(),
    )
    out_specs = (P(("row", "col"), None), P("row", "col", None))
    return jax.shard_map(
        on_device, mesh=mesh, in_specs=in_specs, out_specs=out_specs, check_vma=False
    )
```

profile of v0, /device:TPU:0, one launch (start us, length us, event | category | flops | bytes accessed | tf_op | source)
XLA Modules:
  0.0 683.4 jit_solution(7673028879875781972)
XLA Ops:
  12.8 195.2 %all-gather.2.cloned.1.call-done = bf16[2048,384]{1,0:T(8,128)(2,1)} async-done(((bf16[16,384]{1,0:T(8,128)(2,1)}), bf16[2048,384]{1,0:T(8,128)(2,1)}) %all-gather.2.cloned.1.call-update) | async-done | bytes 1572880 | tf_op jit(solution)/shard_map/all_gather | solution.py:64
  221.2 249.4 %while.13 = (s32[]{:T(128)}, bf16[8,32,128,128]{3,2,1,0:T(8,128)(2,1)}, f32[8,16,32,128]{3,2,1,0:T(8,128)}, s32[8]{0:T(128)S(1)}, bf16[256,128,128]{2,1,0:T(8,12...) while((s32[]{:T(128)}, ...), condition=%wide.region_11.12_spmd.clone, body=%wide.region_6.11_spmd.clone.sunk | while | flops 1692082432 | bytes 61893216 | solution.py:123
  228.0 2.4 multiply_reduce_fusion.2
  232.8 4.5 fusion.118
  237.3 8.0 %fusion.119 = f32[4096,128]{1,0:T(8,128)} fusion(bf16[512,128]{1,0:T(8,128)(2,1)} %get-tuple-element.388, f32[4096,512]{1,0:T(8,128)} %fusion.118, bf16[4096,128]{1,0:T(8,128)(2,1)S(1)} %bitcast.113, bf16[128,512]{1,0:T(8,128)(2,1)} %get-tuple-element.387), kind=kOutput, calls=%fused_computation.13.clone.1 | convolution fusion | flops 1086324736 | bytes 11796480 | tf_op jit(solution)/shard_map/while/body/eval_jaxpr/dot_general | solution.py:18
  245.3 2.5 convert_reduce_fusion.5
  259.1 2.4 multiply_reduce_fusion.2
  264.0 4.5 fusion.118
  268.4 8.0 %fusion.119 = f32[4096,128]{1,0:T(8,128)} fusion(bf16[512,128]{1,0:T(8,128)(2,1)} %get-tuple-element.388, f32[4096,512]{1,0:T(8,128)} %fusion.118, bf16[4096,128]{1,0:T(8,128)(2,1)S(1)} %bitcast.113, bf16[128,512]{1,0:T(8,128)(2,1)} %get-tuple-element.387), kind=kOutput, calls=%fused_computation.13.clone.1 | convolution fusion | flops 1086324736 | bytes 11796480 | tf_op jit(solution)/shard_map/while/body/eval_jaxpr/dot_general | solution.py:18
  276.5 2.5 convert_reduce_fusion.5
  290.3 2.4 multiply_reduce_fusion.2
  295.1 4.5 fusion.118
  299.6 8.0 %fusion.119 = f32[4096,128]{1,0:T(8,128)} fusion(bf16[512,128]{1,0:T(8,128)(2,1)} %get-tuple-element.388, f32[4096,512]{1,0:T(8,128)} %fusion.118, bf16[4096,128]{1,0:T(8,128)(2,1)S(1)} %bitcast.113, bf16[128,512]{1,0:T(8,128)(2,1)} %get-tuple-element.387), kind=kOutput, calls=%fused_computation.13.clone.1 | convolution fusion | flops 1086324736 | bytes 11796480 | tf_op jit(solution)/shard_map/while/body/eval_jaxpr/dot_general | solution.py:18
  307.6 2.5 convert_reduce_fusion.5
  326.3 4.5 fusion.118
  330.7 8.0 %fusion.119 = f32[4096,128]{1,0:T(8,128)} fusion(bf16[512,128]{1,0:T(8,128)(2,1)} %get-tuple-element.388, f32[4096,512]{1,0:T(8,128)} %fusion.118, bf16[4096,128]{1,0:T(8,128)(2,1)S(1)} %bitcast.113, bf16[128,512]{1,0:T(8,128)(2,1)} %get-tuple-element.387), kind=kOutput, calls=%fused_computation.13.clone.1 | convolution fusion | flops 1086324736 | bytes 11796480 | tf_op jit(solution)/shard_map/while/body/eval_jaxpr/dot_general | solution.py:18
  338.8 2.5 convert_reduce_fusion.5
  357.4 4.5 fusion.118
  361.9 8.0 %fusion.119 = f32[4096,128]{1,0:T(8,128)} fusion(bf16[512,128]{1,0:T(8,128)(2,1)} %get-tuple-element.388, f32[4096,512]{1,0:T(8,128)} %fusion.118, bf16[4096,128]{1,0:T(8,128)(2,1)S(1)} %bitcast.113, bf16[128,512]{1,0:T(8,128)(2,1)} %get-tuple-element.387), kind=kOutput, calls=%fused_computation.13.clone.1 | convolution fusion | flops 1086324736 | bytes 11796480 | tf_op jit(solution)/shard_map/while/body/eval_jaxpr/dot_general | solution.py:18
  369.9 2.5 convert_reduce_fusion.5
  388.6 4.5 fusion.118
  393.0 8.0 %fusion.119 = f32[4096,128]{1,0:T(8,128)} fusion(bf16[512,128]{1,0:T(8,128)(2,1)} %get-tuple-element.388, f32[4096,512]{1,0:T(8,128)} %fusion.118, bf16[4096,128]{1,0:T(8,128)(2,1)S(1)} %bitcast.113, bf16[128,512]{1,0:T(8,128)(2,1)} %get-tuple-element.387), kind=kOutput, calls=%fused_computation.13.clone.1 | convolution fusion | flops 1086324736 | bytes 11796480 | tf_op jit(solution)/shard_map/while/body/eval_jaxpr/dot_general | solution.py:18
  401.1 2.5 convert_reduce_fusion.5
  419.7 4.5 fusion.118
  424.2 8.0 %fusion.119 = f32[4096,128]{1,0:T(8,128)} fusion(bf16[512,128]{1,0:T(8,128)(2,1)} %get-tuple-element.388, f32[4096,512]{1,0:T(8,128)} %fusion.118, bf16[4096,128]{1,0:T(8,128)(2,1)S(1)} %bitcast.113, bf16[128,512]{1,0:T(8,128)(2,1)} %get-tuple-element.387), kind=kOutput, calls=%fused_computation.13.clone.1 | convolution fusion | flops 1086324736 | bytes 11796480 | tf_op jit(solution)/shard_map/while/body/eval_jaxpr/dot_general | solution.py:18
  432.2 2.5 convert_reduce_fusion.5
  450.9 4.5 fusion.118
  455.3 8.0 %fusion.119 = f32[4096,128]{1,0:T(8,128)} fusion(bf16[512,128]{1,0:T(8,128)(2,1)} %get-tuple-element.388, f32[4096,512]{1,0:T(8,128)} %fusion.118, bf16[4096,128]{1,0:T(8,128)(2,1)S(1)} %bitcast.113, bf16[128,512]{1,0:T(8,128)(2,1)} %get-tuple-element.387), kind=kOutput, calls=%fused_computation.13.clone.1 | convolution fusion | flops 1086324736 | bytes 11796480 | tf_op jit(solution)/shard_map/while/body/eval_jaxpr/dot_general | solution.py:18
  463.4 2.5 convert_reduce_fusion.5
  473.0 66.9 %pmax.7 = f32[8,16,32]{2,1,0:T(8,128)S(1)} all-reduce(f32[8,16,32]{2,1,0:T(8,128)S(1)} %reduce_max.9), channel_id=1, replica_groups=mesh['row'=8,'col'=16] {'col'}, use_global_device_ids=true, to_apply=%region_13.14 | all-reduce | flops 4096 | bytes 32768 | tf_op jit(solution)/shard_map/pmax | solution.py:126
  545.7 33.7 %psum.15 = bf16[256,16]{0,1:T(8,128)(2,1)S(1)} all-reduce(bf16[256,16]{0,1:T(8,128)(2,1)S(1)} %convert_element_type.127), channel_id=1, replica_groups=mesh['row'=8,'col'=16] {'col'}, use_global_device_ids=true, to_apply=%region_16.17 | all-reduce | flops 4096 | bytes 16384 | tf_op jit(solution)/shard_map/psum | solution.py:139
  579.8 95.1 %all-reduce.2.cloned.1.call-done = bf16[256,384]{1,0:T(8,128)(2,1)} async-done(((bf16[256,384]{1,0:T(8,128)(2,1)}), bf16[256,384]{1,0:T(8,128)(2,1)}) %all-reduce.2.cloned.1.call-update) | async-done | bytes 196624 | tf_op jit(solution)/shard_map/psum | solution.py:138
  (393 shorter events, 132.2 us)
Async XLA Ops:
  7.2 211.5 %copy-start = (bf16[384,384]{1,0:T(8,128)(2,1)S(1)}, bf16[384,384]{1,0:T(8,128)(2,1)}, u32[]{:S(2)}) copy-start(bf16[384,384]{1,0:T(8,128)(2,1)} %param.33) | copy-start | bytes 884740
  7.2 209.2 %copy-start.9 = (bf16[1024,128]{1,0:T(8,128)(2,1)S(1)}, bf16[1024,128]{1,0:T(8,128)(2,1)}, u32[]{:S(2)}) copy-start(bf16[1024,128]{1,0:T(8,128)(2,1)} %param.26) | copy-start | bytes 786436
  7.2 200.8 %all-gather.2.cloned.1.call-start = ((), (), s32[]{:S(2)}) async-start(), calls=%async_computation | async-start | bytes 1585152 | tf_op jit(solution)/shard_map/all_gather | solution.py:64
  7.9 666.9 %all-reduce.2.cloned.1.call-start = ((), (), s32[]{:S(2)}) async-start(), calls=%async_computation.1 | async-start | bytes 393216 | tf_op jit(solution)/shard_map/psum | solution.py:138
  214.4 4.4 copy-start.15
  216.4 3.6 copy-start.20
  245.3 3.9 copy-start.21
  245.3 3.9 copy-start.22
  252.6 3.5 copy-start.11
  252.6 3.5 copy-start.23
  276.4 3.9 copy-start.21
  276.5 3.9 copy-start.22
  307.6 3.9 copy-start.21
  307.6 3.9 copy-start.22
  314.9 3.5 copy-start.11
  338.7 3.9 copy-start.21
  338.8 3.9 copy-start.22
  369.9 3.9 copy-start.21
  369.9 3.9 copy-start.22
  401.0 3.9 copy-start.21
  401.0 3.9 copy-start.22
  432.2 3.9 copy-start.21
  432.2 3.9 copy-start.22
  463.3 3.9 copy-start.21
  463.3 3.9 copy-start.22
  470.6 69.3 %copy-start.3 = (f32[8,16,32,128]{3,2,1,0:T(8,128)S(1)}, f32[8,16,32,128]{3,2,1,0:T(8,128)}, u32[]{:S(2)}) copy-start(f32[8,16,32,128]{3,2,1,0:T(8,128)} %get-tuple-element.85) | copy-start | bytes 6291460
  473.0 68.2 %copy-start.6 = (bf16[128,384]{0,1:T(8,128)(2,1)S(1)}, bf16[128,384]{0,1:T(8,128)(2,1)}, u32[]{:S(2)}) copy-start(bf16[128,384]{0,1:T(8,128)(2,1)} %copy.42) | copy-start | bytes 294916
  542.7 132.2 %copy-start.7 = (bf16[384,384]{1,0:T(8,128)(2,1)S(1)}, bf16[384,384]{1,0:T(8,128)(2,1)}, u32[]{:S(2)}) copy-start(bf16[384,384]{1,0:T(8,128)(2,1)} %param.37) | copy-start | bytes 884740
  542.7 132.2 %copy-start.8 = (bf16[384,384]{1,0:T(8,128)(2,1)S(1)}, bf16[384,384]{1,0:T(8,128)(2,1)}, u32[]{:S(2)}) copy-start(bf16[384,384]{1,0:T(8,128)(2,1)} %param.36) | copy-start | bytes 884740
  542.7 132.1 %copy-start.10 = (bf16[16,384]{1,0:T(8,128)(2,1)S(1)}, bf16[16,384]{1,0:T(8,128)(2,1)}, u32[]{:S(2)}) copy-start(bf16[16,384]{1,0:T(8,128)(2,1)} %param.20) | copy-start | bytes 36868
  542.7 132.1 %copy-start.16 = (f32[384]{0:T(512)S(1)}, f32[384]{0:T(512)}, u32[]{:S(2)}) copy-start(f32[384]{0:T(512)} %param.23) | copy-start | bytes 4612
  542.7 132.1 %copy-start.18 = (f32[16]{0:T(128)S(1)}, f32[16]{0:T(128)}, u32[]{:S(2)}) copy-start(f32[16]{0:T(128)} %copy-done.17) | copy-start | bytes 196
  (79 other events, 238.4 us)
Sparse Core Ops, SparseCore 0:
  9.7 198.2 all-gather.1
  545.7 129.0 all-reduce.1
where the time goes:
time: 685 us; the launch traced here: 683 us
  waiting for transfers between devices  291 us (42%)
  matrix products  132 us (19%)
  other arithmetic  101 us (15%)
  blocking collectives  101 us (15%)
  local copies, waits for them, and re-layouts  26.2 us (4%)
  loops' own time  18.1 us (3%)
  between operations  15 us (2%)
    all_gather x1, waiting for transfers between devices, on_device(): everything = lax.all_gather(single, ('row', 'col'), axis=0, tiled=True)  195 us
    dot_general x37, matrix products, matmul(): return jnp.dot(left_side, right_side, preferred_element_type=jnp.float32)  121 us
    psum x1, waiting for transfers between devices, on_device(): lax.psum(numerator.astype(jnp.bfloat16), 'col').astype(jnp.float32)  95.1 us
    pmax x1, blocking collectives, on_device(): row_peak = lax.pmax(local_peak, 'col')  66.9 us
    reduce_sum x19, other arithmetic, normalize(): average = jnp.mean(values, -1, keepdims=True)  39.9 us
    psum x1, blocking collectives, on_device(): lax.psum(denominator.astype(jnp.bfloat16), 'col').astype(jnp.float32)  33.7 us
    reduce_sum x19, other arithmetic, normalize(): variance = jnp.mean(centered * centered, -1, keepdims=True)  33.2 us
    convert_element_type x8, other arithmetic, one_block(): normed = normalize(middle, pair_gain).astype(jnp.bfloat16).reshape(block_...  19 us
  transfers between devices with their start and end apart: 2, of which 2 were waited for; matrix products, arithmetic and copies ran while one was open for 1% of the time, Pallas kernels for 0%

commit v1 on v0

--- a/solution.py
+++ b/solution.py
@@ -61,7 +61,10 @@
 
     own_norm = normalize(single.astype(jnp.float32), single_gain).astype(jnp.bfloat16)
     gate_lin = matmul(own_norm, w_gate_attn)
-    everything = lax.all_gather(single, ("row", "col"), axis=0, tiled=True)
+    everything = jnp.concatenate(
+        lax.all_to_all(jnp.stack([single] * lax.axis_size(("row", "col"))), ("row", "col"), 0, 0),
+        axis=0,
+    )
     row_norm = normalize(
         lax.dynamic_slice_in_dim(everything, row_start, row_count, 0).astype(jnp.float32),
         single_gain,

time: 685 us -> 515 us (0.75)
  waiting for transfers between devices: 291 us -> 115 us
  starting transfers between devices: 0.08 us -> 11.2 us
    all_gather x1 -> x0, waiting for transfers between devices: 195 us -> none  [on_device(): everything = lax.all_gather(single, ('row', 'col'), axis=0, tiled=True)]
    all_to_all x0 -> x1, waiting for transfers between devices: none -> 20.8 us  [on_device(): lax.all_to_all(jnp.stack([single] * lax.axis_size(('row', 'col'))), ('row...]
    all_to_all x0 -> x1, starting transfers between devices: none -> 11.2 us  [on_device(): lax.all_to_all(jnp.stack([single] * lax.axis_size(('row', 'col'))), ('row...]
  transfers between devices with their start and end apart: 2 -> 2, of which waited for: 2 -> 2; matrix products, arithmetic and copies ran while one was open for 1% -> 0% of each run, Pallas kernels for 0% -> 0%
where the time goes in v1:
time: 515 us; the launch traced here: 513 us
  matrix products  130 us (25%)
  waiting for transfers between devices  115 us (22%)
  blocking collectives  101 us (20%)
  other arithmetic  95.3 us (19%)
  local copies, waits for them, and re-layouts  27 us (5%)
  loops' own time  18.3 us (4%)
  between operations  15.1 us (3%)
  starting transfers between devices  11.2 us (2%)
    dot_general x37, matrix products, matmul(): return jnp.dot(left_side, right_side, preferred_element_type=jnp.float32)  119 us
    psum x1, waiting for transfers between devices, on_device(): lax.psum(numerator.astype(jnp.bfloat16), 'col').astype(jnp.float32)  94.6 us
    pmax x1, blocking collectives, on_device(): row_peak = lax.pmax(local_peak, 'col')  67.5 us
    reduce_sum x19, other arithmetic, normalize(): average = jnp.mean(values, -1, keepdims=True)  37.4 us
    psum x1, blocking collectives, on_device(): lax.psum(denominator.astype(jnp.bfloat16), 'col').astype(jnp.float32)  33.7 us
    reduce_sum x19, other arithmetic, normalize(): variance = jnp.mean(centered * centered, -1, keepdims=True)  30.6 us
    all_to_all x1, waiting for transfers between devices, on_device(): lax.all_to_all(jnp.stack([single] * lax.axis_size(('row', 'col'))), ('row...  20.8 us
    convert_element_type x8, other arithmetic, one_block(): normed = normalize(middle, pair_gain).astype(jnp.bfloat16).reshape(block_...  19 us
  transfers between devices with their start and end apart: 2, of which 2 were waited for; matrix products, arithmetic and copies ran while one was open for 0% of the time, Pallas kernels for 0%

profile of v1, /device:TPU:0, one launch (start us, length us, event | category | flops | bytes accessed | tf_op | source)
XLA Modules:
  0.0 513.3 jit_solution(5963061855101235303)
XLA Ops:
  9.3 11.2 %all-to-all-start = ((bf16[128,16,384]{2,1,0:T(8,128)(2,1)}), bf16[128,16,384]{2,1,0:T(8,128)(2,1)S(1)}, u32[]{:S(2)}, u32[]{:S(2)}) async-start(bf16[128,16,384]{2,1,0:T(8,128)(2,1)} %stack.2), calls=%async_computation | async-start | bytes 3145728 | tf_op jit(solution)/shard_map/all_to_all | solution.py:65
  22.7 20.8 %all-to-all-done = bf16[128,16,384]{2,1,0:T(8,128)(2,1)S(1)} async-done(((bf16[128,16,384]{2,1,0:T(8,128)(2,1)}), bf16[128,16,384]{2,1,0:T(8,128)(2,1)S(1)}, u32[]{:S(2)}, u32[]{:S(2)}) %all-to-all-start) | async-done | bytes 1572896 | tf_op jit(solution)/shard_map/all_to_all | solution.py:65
  51.1 249.3 %while.13 = (s32[]{:T(128)}, bf16[8,32,128,128]{3,2,1,0:T(8,128)(2,1)}, f32[8,16,32,128]{3,2,1,0:T(8,128)}, s32[8]{0:T(128)S(1)}, bf16[256,128,128]{2,1,0:T(8,12...) while((s32[]{:T(128)}, ...), condition=%wide.region_11.12_spmd.clone, body=%wide.region_6.11_spmd.clone.sunk | while | flops 1692082432 | bytes 62022272 | solution.py:126
  62.7 4.5 fusion.118
  67.1 8.0 %fusion.119 = f32[4096,128]{1,0:T(8,128)} fusion(bf16[512,128]{1,0:T(8,128)(2,1)} %get-tuple-element.405, f32[4096,512]{1,0:T(8,128)} %fusion.118, bf16[4096,128]{1,0:T(8,128)(2,1)S(1)} %bitcast.114, bf16[128,512]{1,0:T(8,128)(2,1)} %get-tuple-element.404), kind=kOutput, calls=%fused_computation.13.clone.1 | convolution fusion | flops 1086324736 | bytes 11796480 | tf_op jit(solution)/shard_map/while/body/eval_jaxpr/dot_general | solution.py:18
  75.2 2.5 convert_reduce_fusion.5
  89.0 2.4 multiply_reduce_fusion.2
  93.8 4.5 fusion.118
  98.3 8.0 %fusion.119 = f32[4096,128]{1,0:T(8,128)} fusion(bf16[512,128]{1,0:T(8,128)(2,1)} %get-tuple-element.405, f32[4096,512]{1,0:T(8,128)} %fusion.118, bf16[4096,128]{1,0:T(8,128)(2,1)S(1)} %bitcast.114, bf16[128,512]{1,0:T(8,128)(2,1)} %get-tuple-element.404), kind=kOutput, calls=%fused_computation.13.clone.1 | convolution fusion | flops 1086324736 | bytes 11796480 | tf_op jit(solution)/shard_map/while/body/eval_jaxpr/dot_general | solution.py:18
  106.3 2.5 convert_reduce_fusion.5
  120.1 2.4 multiply_reduce_fusion.2
  124.9 4.5 fusion.118
  129.4 8.0 %fusion.119 = f32[4096,128]{1,0:T(8,128)} fusion(bf16[512,128]{1,0:T(8,128)(2,1)} %get-tuple-element.405, f32[4096,512]{1,0:T(8,128)} %fusion.118, bf16[4096,128]{1,0:T(8,128)(2,1)S(1)} %bitcast.114, bf16[128,512]{1,0:T(8,128)(2,1)} %get-tuple-element.404), kind=kOutput, calls=%fused_computation.13.clone.1 | convolution fusion | flops 1086324736 | bytes 11796480 | tf_op jit(solution)/shard_map/while/body/eval_jaxpr/dot_general | solution.py:18
  137.4 2.5 convert_reduce_fusion.5
  156.1 4.5 fusion.118
  160.5 8.0 %fusion.119 = f32[4096,128]{1,0:T(8,128)} fusion(bf16[512,128]{1,0:T(8,128)(2,1)} %get-tuple-element.405, f32[4096,512]{1,0:T(8,128)} %fusion.118, bf16[4096,128]{1,0:T(8,128)(2,1)S(1)} %bitcast.114, bf16[128,512]{1,0:T(8,128)(2,1)} %get-tuple-element.404), kind=kOutput, calls=%fused_computation.13.clone.1 | convolution fusion | flops 1086324736 | bytes 11796480 | tf_op jit(solution)/shard_map/while/body/eval_jaxpr/dot_general | solution.py:18
  168.5 2.5 convert_reduce_fusion.5
  187.2 4.5 fusion.118
  191.7 8.0 %fusion.119 = f32[4096,128]{1,0:T(8,128)} fusion(bf16[512,128]{1,0:T(8,128)(2,1)} %get-tuple-element.405, f32[4096,512]{1,0:T(8,128)} %fusion.118, bf16[4096,128]{1,0:T(8,128)(2,1)S(1)} %bitcast.114, bf16[128,512]{1,0:T(8,128)(2,1)} %get-tuple-element.404), kind=kOutput, calls=%fused_computation.13.clone.1 | convolution fusion | flops 1086324736 | bytes 11796480 | tf_op jit(solution)/shard_map/while/body/eval_jaxpr/dot_general | solution.py:18
  199.7 2.5 convert_reduce_fusion.5
  218.3 4.5 fusion.118
  222.8 8.0 %fusion.119 = f32[4096,128]{1,0:T(8,128)} fusion(bf16[512,128]{1,0:T(8,128)(2,1)} %get-tuple-element.405, f32[4096,512]{1,0:T(8,128)} %fusion.118, bf16[4096,128]{1,0:T(8,128)(2,1)S(1)} %bitcast.114, bf16[128,512]{1,0:T(8,128)(2,1)} %get-tuple-element.404), kind=kOutput, calls=%fused_computation.13.clone.1 | convolution fusion | flops 1086324736 | bytes 11796480 | tf_op jit(solution)/shard_map/while/body/eval_jaxpr/dot_general | solution.py:18
  230.8 2.5 convert_reduce_fusion.5
  249.5 4.5 fusion.118
  254.0 8.0 %fusion.119 = f32[4096,128]{1,0:T(8,128)} fusion(bf16[512,128]{1,0:T(8,128)(2,1)} %get-tuple-element.405, f32[4096,512]{1,0:T(8,128)} %fusion.118, bf16[4096,128]{1,0:T(8,128)(2,1)S(1)} %bitcast.114, bf16[128,512]{1,0:T(8,128)(2,1)} %get-tuple-element.404), kind=kOutput, calls=%fused_computation.13.clone.1 | convolution fusion | flops 1086324736 | bytes 11796480 | tf_op jit(solution)/shard_map/while/body/eval_jaxpr/dot_general | solution.py:18
  262.0 2.5 convert_reduce_fusion.5
  280.6 4.5 fusion.118
  285.1 8.0 %fusion.119 = f32[4096,128]{1,0:T(8,128)} fusion(bf16[512,128]{1,0:T(8,128)(2,1)} %get-tuple-element.405, f32[4096,512]{1,0:T(8,128)} %fusion.118, bf16[4096,128]{1,0:T(8,128)(2,1)S(1)} %bitcast.114, bf16[128,512]{1,0:T(8,128)(2,1)} %get-tuple-element.404), kind=kOutput, calls=%fused_computation.13.clone.1 | convolution fusion | flops 1086324736 | bytes 11796480 | tf_op jit(solution)/shard_map/while/body/eval_jaxpr/dot_general | solution.py:18
  293.1 2.5 convert_reduce_fusion.5
  302.7 67.5 %pmax.7 = f32[8,16,32]{2,1,0:T(8,128)S(1)} all-reduce(f32[8,16,32]{2,1,0:T(8,128)S(1)} %reduce_max.9), channel_id=1, replica_groups=mesh['row'=8,'col'=16] {'col'}, use_global_device_ids=true, to_apply=%region_13.14 | all-reduce | flops 4096 | bytes 32768 | tf_op jit(solution)/shard_map/pmax | solution.py:129
  376.1 33.7 %psum.15 = bf16[256,16]{0,1:T(8,128)(2,1)S(1)} all-reduce(bf16[256,16]{0,1:T(8,128)(2,1)S(1)} %convert_element_type.127), channel_id=1, replica_groups=mesh['row'=8,'col'=16] {'col'}, use_global_device_ids=true, to_apply=%region_16.17 | all-reduce | flops 4096 | bytes 16384 | tf_op jit(solution)/shard_map/psum | solution.py:142
  410.1 94.6 %all-reduce.2.cloned.1.call-done = bf16[256,384]{1,0:T(8,128)(2,1)} async-done(((bf16[256,384]{1,0:T(8,128)(2,1)}), bf16[256,384]{1,0:T(8,128)(2,1)}) %all-reduce.2.cloned.1.call-update) | async-done | bytes 196624 | tf_op jit(solution)/shard_map/psum | solution.py:141
  (421 shorter events, 127.2 us)
Async XLA Ops:
  7.2 41.4 %copy-start = (bf16[384,384]{1,0:T(8,128)(2,1)S(1)}, bf16[384,384]{1,0:T(8,128)(2,1)}, u32[]{:S(2)}) copy-start(bf16[384,384]{1,0:T(8,128)(2,1)} %param.33) | copy-start | bytes 884740
  7.2 14.7 %copy-start.11 = (bf16[16,384]{1,0:T(8,128)(2,1)S(1)}, bf16[16,384]{1,0:T(8,128)(2,1)}, u32[]{:S(2)}) copy-start(bf16[16,384]{1,0:T(8,128)(2,1)} %param.20) | copy-start | bytes 36868
  7.2 13.3 %copy-start.28 = (s32[8]{0:T(128)S(1)}, s32[8]{0:T(128)}, u32[]{:S(2)}) copy-start(s32[8]{0:T(128)} %param.22) | copy-start | bytes 100
  9.2 35.0 %copy-start.19 = (f32[384]{0:T(512)S(1)}, f32[384]{0:T(512)}, u32[]{:S(2)}) copy-start(f32[384]{0:T(512)} %param.23) | copy-start | bytes 4612
  9.3 35.0 %copy-start.24 = (bf16[384,384]{1,0:T(8,128)(2,1)S(1)}, bf16[384,384]{1,0:T(8,128)(2,1)}, u32[]{:S(2)}) copy-start(bf16[384,384]{1,0:T(8,128)(2,1)} %param.34) | copy-start | bytes 884740
  9.3 36.0 %copy-start.25 = (bf16[384,384]{1,0:T(8,128)(2,1)S(1)}, bf16[384,384]{1,0:T(8,128)(2,1)}, u32[]{:S(2)}) copy-start(bf16[384,384]{1,0:T(8,128)(2,1)} %param.35) | copy-start | bytes 884740
  9.3 37.0 %copy-start.10 = (bf16[1024,128]{1,0:T(8,128)(2,1)S(1)}, bf16[1024,128]{1,0:T(8,128)(2,1)}, u32[]{:S(2)}) copy-start(bf16[1024,128]{1,0:T(8,128)(2,1)} %param.26) | copy-start | bytes 786436
  9.3 37.0 %copy-start.16 = (bf16[384,32]{0,1:T(8,128)(2,1)S(1)}, bf16[384,32]{0,1:T(8,128)(2,1)}, u32[]{:S(2)}) copy-start(bf16[384,32]{0,1:T(8,128)(2,1)} %param.25) | copy-start | bytes 73732
  9.3 34.3 %all-to-all-start = ((bf16[128,16,384]{2,1,0:T(8,128)(2,1)}), bf16[128,16,384]{2,1,0:T(8,128)(2,1)S(1)}, u32[]{:S(2)}, u32[]{:S(2)}) async-start(bf16[128,16,384]{2,1,0:T(8,128)(2,1)} %stack.2), calls=%async_computation | async-start | bytes 3145728 | tf_op jit(solution)/shard_map/all_to_all | solution.py:65
  20.5 484.3 %all-reduce.2.cloned.1.call-start = ((), (), s32[]{:S(2)}) async-start(), calls=%async_computation.1 | async-start | bytes 393216 | tf_op jit(solution)/shard_map/psum | solution.py:141
  22.0 21.8 %copy-start.21 = (f32[16]{0:T(128)}, f32[16]{0:T(128)S(1)}, u32[]{:S(2)}) copy-start(f32[16]{0:T(128)S(1)} %broadcast_multiply_fusion.4) | copy-start | bytes 196
  46.3 4.8 copy-start.17
  75.1 3.9 copy-start.27
  75.1 3.9 copy-start.29
  106.3 3.9 copy-start.27
  106.3 3.9 copy-start.29
  137.4 3.9 copy-start.27
  137.4 3.9 copy-start.29
  168.5 3.9 copy-start.29
  199.7 3.9 copy-start.27
  199.7 3.9 copy-start.29
  230.8 3.9 copy-start.29
  262.0 3.9 copy-start.27
  262.0 3.9 copy-start.29
  293.1 3.9 copy-start.27
  293.1 3.9 copy-start.29
  300.4 69.9 %copy-start.3 = (f32[8,16,32,128]{3,2,1,0:T(8,128)S(1)}, f32[8,16,32,128]{3,2,1,0:T(8,128)}, u32[]{:S(2)}) copy-start(f32[8,16,32,128]{3,2,1,0:T(8,128)} %get-tuple-element.85) | copy-start | bytes 6291460
  302.7 68.8 %copy-start.7 = (bf16[128,384]{0,1:T(8,128)(2,1)S(1)}, bf16[128,384]{0,1:T(8,128)(2,1)}, u32[]{:S(2)}) copy-start(bf16[128,384]{0,1:T(8,128)(2,1)} %copy.52) | copy-start | bytes 294916
  373.0 131.7 %copy-start.8 = (bf16[384,384]{1,0:T(8,128)(2,1)S(1)}, bf16[384,384]{1,0:T(8,128)(2,1)}, u32[]{:S(2)}) copy-start(bf16[384,384]{1,0:T(8,128)(2,1)} %param.37) | copy-start | bytes 884740
  373.1 131.7 %copy-start.9 = (bf16[384,384]{1,0:T(8,128)(2,1)S(1)}, bf16[384,384]{1,0:T(8,128)(2,1)}, u32[]{:S(2)}) copy-start(bf16[384,384]{1,0:T(8,128)(2,1)} %param.36) | copy-start | bytes 884740
  373.1 131.7 %copy-start.20 = (f32[384]{0:T(512)S(1)}, f32[384]{0:T(512)}, u32[]{:S(2)}) copy-start(f32[384]{0:T(512)} %param.23) | copy-start | bytes 4612
  373.1 131.7 %copy-start.22 = (f32[16]{0:T(128)S(1)}, f32[16]{0:T(128)}, u32[]{:S(2)}) copy-start(f32[16]{0:T(128)} %copy-done.21) | copy-start | bytes 196
  (93 other events, 296.7 us)
Sparse Core Ops, SparseCore 0:
  376.0 128.6 all-reduce.1
